TPU v7x, 32 devices: a whole 2x2x4 slice. The times are simulated.
32 devices in a mesh: row: 4 (over y, core), col: 8 (over z, x).
Axes of the slice: x: 2, y: 2, z: 4, core: 2. Of those that a mesh axis runs over, the one named last changes fastest.
Arguments:
- shell_velocity: bfloat16 [256, 128, 128], P(('row', 'col')), may hold values from -6 to 6
- coupling: bfloat16 [256, 2, 2, 256, 128], P(('row', 'col')), may hold values from -0.375 to 0.375
- coupling_dest: int32 [256, 2], P(('row', 'col')), may hold values from 0 to 7, all different within a row; in each aligned block of 8 rows (0 to 7, 8 to 15, ...) at most 2 rows name the same one
- coupling_cluster: int32 [256, 2], P(('row', 'col')), may hold values from 0 to 63
- near_blocks: bfloat16 [4, 8, 32, 2, 256, 256], P('row', 'col'), may hold values from -0.0625 to 0.0625
- far_v: bfloat16 [4, 8, 64, 2, 32, 256], P('row', 'col'), may hold values from -0.25 to 0.25
- far_u: bfloat16 [4, 8, 64, 2, 32, 256], P('row', 'col'), may hold values from -0.125 to 0.125
- block_pairs: int32 [4, 8, 96], P('row', 'col'), may hold values from 0 to 1023, as said below
Outputs:
- response: bfloat16 [16384, 128], P(('row', 'col'))
Inputs may be any that keep to these rules, and one draw needn't show every extreme that they name: `coupling_dest`: the rows of one device name any column group at most 2 times, and some device names one exactly 2 times; the 2 entries of a row differ. `block_pairs`: each entry codes a row cluster r and column cluster c of its group as r * 64 + c; the entries of one group are distinct.
All inputs are finite; a program needn't handle non-finite values.
Results may differ from a plain program's by a relative error of at most 0.008.
Values may be sent and summed in bfloat16 or wider, within the bound.
A program may use at most 128 MiB of HBM per device.

v0:
```python
import jax
import jax.numpy as jnp
from jax import lax
from jax.sharding import PartitionSpec as P

RC_DEV = 16
CC_DEV = 64
NEAR_DEV = 32


def rotate_blocks(values, load_count):
    return jnp.concatenate([-values[..., load_count:], values[..., :load_count]], axis=-1)


def per_device(
    shell_velocity,
    coupling,
    coupling_dest,
    coupling_cluster,
    near_blocks,
    far_v,
    far_u,
    block_pairs,
):
    width = shell_velocity.shape[-1]
    load_count = width // 2
    shell_count = shell_velocity.shape[0]
    top_count = coupling.shape[1]
    panels = coupling.shape[3]
    contributions = jnp.einsum(
        "stpq,sqk->stpk", coupling[:, :, 0], shell_velocity, preferred_element_type=jnp.float32
    )
    contributions = contributions + jnp.einsum(
        "stpq,sqk->stpk",
        coupling[:, :, 1],
        rotate_blocks(shell_velocity, load_count),
        preferred_element_type=jnp.float32,
    )
    entries = shell_count * top_count
    flat_rows = contributions.astype(jnp.bfloat16).reshape(entries, panels * width)
    col_count = lax.axis_size("col")
    capacity = max(2, (entries + col_count - 1) // col_count)
    target = coupling_dest.reshape(entries)
    target_cluster = coupling_cluster.reshape(entries)
    onehot = (target[:, None] == jnp.arange(col_count, dtype=jnp.int32)[None, :]).astype(jnp.int32)
    before = jnp.cumsum(onehot, axis=0) - onehot
    slot_rank = jnp.sum(before * onehot, axis=1)
    slot_index = target * capacity + slot_rank
    slot_pick = jnp.arange(col_count * capacity, dtype=jnp.int32)[:, None] == slot_index[None, :]
    outgoing = jnp.dot(
        slot_pick.astype(jnp.bfloat16), flat_rows, preferred_element_type=jnp.float32
    )
    outgoing = outgoing.astype(jnp.bfloat16).reshape(col_count, capacity, panels, width)
    slot_ids = jnp.sum(slot_pick.astype(jnp.int32) * (target_cluster + 1)[None, :], axis=1) - 1
    slot_ids = slot_ids.reshape(col_count, capacity)
    incoming, got_ids = (
        lax.all_to_all(outgoing, "col", split_axis=0, concat_axis=0, tiled=True),
        lax.all_to_all(slot_ids, "col", split_axis=0, concat_axis=0, tiled=True),
    )
    cluster_pick = (
        jnp.arange(CC_DEV, dtype=jnp.int32)[:, None] == got_ids.reshape(-1)[None, :]
    ).astype(jnp.bfloat16)
    cluster_sums = jnp.dot(
        cluster_pick,
        incoming.reshape(col_count * capacity, panels * width),
        preferred_element_type=jnp.float32,
    ).reshape(CC_DEV, panels, width)
    source_share = lax.psum_scatter(cluster_sums, "row", scatter_dimension=1, tiled=True).astype(
        jnp.bfloat16
    )
    sources = lax.all_gather(source_share, "row", axis=1, tiled=True)
    pair_codes = block_pairs.reshape(-1)
    owners = pair_codes // CC_DEV
    columns = pair_codes % CC_DEV
    nearby_local = near_blocks[0, 0]
    nearby_input = sources[columns[:NEAR_DEV]]
    nearby_contribution = jnp.einsum(
        "dym,dmg->dyg", nearby_local[:, 0], nearby_input, preferred_element_type=jnp.float32
    )
    nearby_contribution = nearby_contribution + jnp.einsum(
        "dym,dmg->dyg",
        nearby_local[:, 1],
        rotate_blocks(nearby_input, load_count),
        preferred_element_type=jnp.float32,
    )
    distant_input = sources[columns[NEAR_DEV:]]
    distant_right_factor = far_v[0, 0]
    expansion_coefficients = jnp.einsum(
        "dyz,dzi->dyi",
        distant_right_factor[:, 0],
        distant_input,
        preferred_element_type=jnp.float32,
    )
    expansion_coefficients = expansion_coefficients + jnp.einsum(
        "dyz,dzi->dyi",
        distant_right_factor[:, 1],
        rotate_blocks(distant_input, load_count),
        preferred_element_type=jnp.float32,
    )
    expansion_coefficients = expansion_coefficients.astype(jnp.bfloat16)
    far_left = far_u[0, 0]
    far_term = jnp.einsum(
        "brp,brk->bpk", far_left[:, 0], expansion_coefficients, preferred_element_type=jnp.float32
    )
    far_term = far_term + jnp.einsum(
        "brp,brk->bpk",
        far_left[:, 1],
        rotate_blocks(expansion_coefficients, load_count),
        preferred_element_type=jnp.float32,
    )
    all_terms = jnp.concatenate([nearby_contribution, far_term], axis=0)
    high_part = all_terms.astype(jnp.bfloat16)
    low_part = (all_terms - high_part.astype(jnp.float32)).astype(jnp.bfloat16)
    owner_pick = (jnp.arange(RC_DEV, dtype=jnp.int32)[:, None] == owners[None, :]).astype(
        jnp.bfloat16
    )
    row_sums = jnp.einsum("ib,bpk->ipk", owner_pick, high_part, preferred_element_type=jnp.float32)
    row_sums = row_sums + jnp.einsum(
        "ib,bpk->ipk", owner_pick, low_part, preferred_element_type=jnp.float32
    )
    row_sums = row_sums.reshape(RC_DEV * panels, width)
    return lax.psum_scatter(row_sums, "col", scatter_dimension=0, tiled=True).astype(jnp.bfloat16)


def solution(mesh):
    return jax.shard_map(
        per_device,
        mesh=mesh,
        in_specs=(
            P(("row", "col"), None, None),
            P(("row", "col"), None, None, None, None),
            P(("row", "col"), None),
            P(("row", "col"), None),
            P("row", "col", None, None, None, None),
            P("row", "col", None, None, None, None),
            P("row", "col", None, None, None, None),
            P("row", "col", None),
        ),
        out_specs=P(("row", "col"), None),
        check_vma=False,
    )
```

profile of v0, /device:TPU:0, one launch (start us, length us, event | category | flops | bytes accessed | tf_op | source)
XLA Modules:
  0.0 330.5 jit_solution(13551763512401435682)
XLA Ops:
  6.5 0.8 broadcast_add_fusion
  7.4 0.1 copy.65
  7.5 0.1 add.78
  7.5 0.8 copy.64
  8.3 0.1 reshape.84
  8.4 0.1 fusion.30
  8.5 0.2 select_reduce_fusion.1
  8.7 0.1 select_reduce_fusion
  8.8 0.7 sub.20
  9.5 7.3 %all-to-all-start = ((s32[8,1,2]{2,1,0:T(1,128)}), s32[8,1,2]{2,1,0:T(1,128)S(1)}, u32[]{:S(2)}, u32[]{:S(2)}) async-start(s32[8,1,2]{2,1,0:T(1,128)} %bitcast.2), calls=%async_computation | async-start | bytes 8192 | tf_op jit(solution)/shard_map/all_to_all | solution.py:58
  16.8 1.2 fusion.46
  17.9 0.1 copy.89
  18.1 0.1 copy.90
  18.3 1.7 fusion.20
  20.0 0.5 fusion.10
  20.4 0.7 fusion.11
  21.1 1.2 copy.96
  22.3 0.9 all-to-all-done
  23.2 5.1 %all-to-all-start.1 = ((bf16[8,2,256,128]{3,2,1,0:T(8,128)(2,1)}), bf16[8,2,256,128]{3,2,1,0:T(8,128)(2,1)S(1)}, u32[]{:S(2)}, u32[]{:S(2)}) async-start(bf16[8,2,256,128]{3,2,1,0:T(8,128)(2,1)} %bitcast.38), calls=%async_computation.1 | async-start | bytes 2097152 | tf_op jit(solution)/shard_map/all_to_all | solution.py:57
  28.3 0.0 reduce-scatter.3.cloned.1.call-start
  28.3 0.5 broadcast.109
  28.9 0.7 reduce.3
  29.5 0.1 eq.66
  29.6 24.1 %all-to-all-done.1 = bf16[8,2,256,128]{3,2,1,0:T(8,128)(2,1)S(1)} async-done(((bf16[8,2,256,128]{3,2,1,0:T(8,128)(2,1)}), bf16[8,2,256,128]{3,2,1,0:T(8,128)(2,1)S(1)}, u32[]{:S(2)}, u32[]{:S(2)}) %all-to-all-start.1) | async-done | bytes 1048608 | tf_op jit(solution)/shard_map/all_to_all | solution.py:57
  53.7 4.6 %fusion.15 = f32[64,256,128]{2,0,1:T(8,128)} fusion(s32[16]{0:T(128)S(1)} %eq.66, bf16[2,8,256,128]{3,2,1,0:T(8,128)(2,1)S(1)} %bitcast.119), kind=kOutput, calls=%fused_computation.32 | convolution fusion | flops 67109888 | bytes 9437248 | tf_op jit(solution)/shard_map/dot_general | solution.py:63
  58.3 0.0 reduce-scatter.3.cloned.1.call-update
  58.4 0.0 all-gather.2.cloned.1.call-start
  58.4 70.3 %reduce-scatter.3.cloned.1.call-done = f32[64,64,128]{2,0,1:T(8,128)} async-done(((f32[64,256,128]{2,0,1:T(8,128)}), f32[64,64,128]{2,0,1:T(8,128)}) %reduce-scatter.3.cloned.1.call-update) | async-done | bytes 2097168 | tf_op jit(solution)/shard_map/reduce_scatter | solution.py:68
  128.7 2.8 convert_element_type.37
  131.5 0.0 all-gather.2.cloned.1.call-update
  131.6 0.2 reduce-scatter.5.cloned.1.call-start
  131.8 1.5 copy.114
  133.4 0.8 copy-done.6
  134.2 1.5 copy.113
  135.6 8.1 %copy.112 = bf16[1,1,32,2,256,256]{5,4,2,3,1,0:T(8,128)(2,1)} copy(bf16[1,1,32,2,256,256]{5,4,3,2,1,0:T(8,128)(2,1)} %param.12) | data formatting | bytes 16777216 | tf_op args[4]
  143.8 0.1 compare_select_fusion
  143.9 22.3 %all-gather.2.cloned.1.call-done = bf16[64,256,128]{2,0,1:T(8,128)(2,1)} async-done(((bf16[64,64,128]{2,0,1:T(8,128)(2,1)}), bf16[64,256,128]{2,0,1:T(8,128)(2,1)}) %all-gather.2.cloned.1.call-update) | async-done | bytes 4194320 | tf_op jit(solution)/shard_map/all_gather | solution.py:71
  166.2 6.8 %copy.73 = bf16[64,256,128]{2,1,0:T(8,128)(2,1)} copy(bf16[64,256,128]{2,0,1:T(8,128)(2,1)} %all-gather.2.cloned.1.call-done) | data formatting | bytes 8388608 | tf_op jit(solution)/shard_map/all_gather | solution.py:71
  173.0 3.1 gather_fusion
  176.1 5.2 %gather_fusion.1 = bf16[64,256,128]{2,1,0:T(8,128)(2,1)} fusion(bf16[64,256,128]{2,1,0:T(8,128)(2,1)} %copy.73, s32[1024]{0:T(1024)S(1)} %pad_clamp_fusion), kind=kCustom, calls=%fused_computation.1 | custom fusion | bytes 8388864 | tf_op jit(solution)/shard_map/gather | solution.py:86
  181.4 2.9 fusion.45
  184.2 1.9 copy.92
  186.1 1.2 neg.13
  187.4 1.9 copy.93
  189.3 4.0 %fusion.1 = f32[32,128,256]{2,1,0:T(8,128)S(1)} fusion(bf16[32,2,256,256]{3,2,0,1:T(8,128)(2,1)} %bitcast.110, bf16[32,256,64]{1,2,0:T(8,128)(2,1)S(1)} %copy.93, bf16[32,256,64]{1,2,0:T(8,128)(2,1)} %neg.13), kind=kOutput, calls=%fused_computation.10 | convolution fusion | flops 541065216 | bytes 10485760 | tf_op jit(solution)/shard_map/dym,dmg->dyg/dot_general | solution.py:80
  193.3 5.8 %add_bitcast_fusion.1 = f32[32,256,128]{1,2,0:T(8,128)} fusion(f32[32,128,256]{2,1,0:T(8,128)S(1)} %fusion.1, bf16[32,256,128]{2,1,0:T(8,128)(2,1)S(1)} %gather_fusion, bf16[32,2,256,256]{3,2,0,1:T(8,128)(2,1)} %bitcast.111), kind=kOutput, calls=%fused_computation.17 | convolution fusion | flops 537919488 | bytes 14680064 | tf_op jit(solution)/shard_map/dym,dmg->dyg/dot_general | solution.py:77
  199.1 2.0 slice_negate_fusion
  201.1 2.3 fusion.3
  203.5 0.8 fusion.12
  204.3 0.2 slice_negate_fusion.1
  204.5 0.5 copy-done.2
  205.1 1.3 fusion.18
  206.4 5.0 %add_bitcast_fusion = f32[64,256,128]{1,2,0:T(8,128)} fusion(f32[64,128,256]{2,1,0:T(8,128)S(1)} %fusion.18, bf16[64,2,32,256]{3,2,0,1:T(8,128)(2,1)S(1)} %bitcast.113, bf16[64,32,64]{2,1,0:T(8,128)(2,1)S(1)} %get-tuple-element.10, bf16[64,32,64]{2,1,0:T(8,128)(2,1)S(1)} %get-tuple-element.9), kind=kOutput, calls=%fused_computation.7 | convolution fusion | flops 137363456 | bytes 18874368 | tf_op jit(solution)/shard_map/brp,brk->bpk/dot_general | solution.py:105
  211.4 9.0 %subtract_convert_fusion = bf16[96,256,128]{1,2,0:T(8,128)(2,1)} fusion(f32[64,256,128]{1,2,0:T(8,128)} %add_bitcast_fusion, f32[32,256,128]{1,2,0:T(8,128)} %add_bitcast_fusion.1), kind=kLoop, calls=%fused_computation.4 | loop fusion | flops 15728640 | bytes 18874368 | tf_op jit(solution)/shard_map/convert_element_type | solution.py:113
  220.4 7.9 %fusion = bf16[96,256,128]{1,2,0:T(8,128)(2,1)} fusion(f32[64,256,128]{1,2,0:T(8,128)} %add_bitcast_fusion, f32[32,256,128]{1,2,0:T(8,128)} %add_bitcast_fusion.1), kind=kLoop, calls=%fused_computation.5 | loop fusion | flops 3145728 | bytes 18874368 | tf_op jit(solution)/shard_map/convert_element_type | solution.py:112
  228.3 9.0 %copy.81 = bf16[96,256,128]{2,0,1:T(8,128)(2,1)} copy(bf16[96,256,128]{1,2,0:T(8,128)(2,1)} %fusion) | data formatting | bytes 12582912 | tf_op jit(solution)/shard_map/convert_element_type | solution.py:112
  237.3 9.1 %copy.82 = bf16[96,256,128]{2,0,1:T(8,128)(2,1)} copy(bf16[96,256,128]{1,2,0:T(8,128)(2,1)} %subtract_convert_fusion) | data formatting | bytes 12582912 | tf_op jit(solution)/shard_map/convert_element_type | solution.py:113
  246.4 3.9 %fusion.33 = f32[16,256,128]{2,0,1:T(8,128)S(1)} fusion(bf16[96,256,128]{2,0,1:T(8,128)(2,1)} %copy.81, s32[96]{0:T(128)S(1)} %get-tuple-element.13), kind=kOutput, calls=%fused_computation.61 | convolution fusion | flops 100664832 | bytes 8388992 | tf_op jit(solution)/shard_map/ib,bpk->ipk/dot_general | solution.py:117
  250.2 0.7 copy-done.1
  251.0 0.9 convolution_add_fusion
  251.9 2.0 copy.83
  253.9 0.0 reduce-scatter.5.cloned.1.call-update
  253.9 68.5 %reduce-scatter.5.cloned.1.call-done = f32[512,128]{1,0:T(8,128)} async-done(((f32[4096,128]{1,0:T(8,128)}), f32[512,128]{1,0:T(8,128)}) %reduce-scatter.5.cloned.1.call-update) | async-done | bytes 262160 | tf_op jit(solution)/shard_map/reduce_scatter | solution.py:122
  322.4 1.6 convert_element_type.43
  (21 shorter events, 0.1 us)
Async XLA Ops:
  6.5 13.4 %copy-start.4 = (bf16[8,2,2,256,128]{4,3,2,1,0:T(8,128)(2,1)S(1)}, bf16[8,2,2,256,128]{4,3,2,1,0:T(8,128)(2,1)}, u32[]{:S(2)}) copy-start(bf16[8,2,2,256,128]{4,3,2,1,0:T(8,128)(2,1)} %param.9) | copy-start | bytes 6291460
  9.5 13.7 %all-to-all-start = ((s32[8,1,2]{2,1,0:T(1,128)}), s32[8,1,2]{2,1,0:T(1,128)S(1)}, u32[]{:S(2)}, u32[]{:S(2)}) async-start(s32[8,1,2]{2,1,0:T(1,128)} %bitcast.2), calls=%async_computation | async-start | bytes 8192 | tf_op jit(solution)/shard_map/all_to_all | solution.py:58
  23.2 30.5 %all-to-all-start.1 = ((bf16[8,2,256,128]{3,2,1,0:T(8,128)(2,1)}), bf16[8,2,256,128]{3,2,1,0:T(8,128)(2,1)S(1)}, u32[]{:S(2)}, u32[]{:S(2)}) async-start(bf16[8,2,256,128]{3,2,1,0:T(8,128)(2,1)} %bitcast.38), calls=%async_computation.1 | async-start | bytes 2097152 | tf_op jit(solution)/shard_map/all_to_all | solution.py:57
  28.3 100.4 %reduce-scatter.3.cloned.1.call-start = ((), (), s32[]{:S(2)}) async-start(), calls=%async_computation.4 | async-start | bytes 10485760 | tf_op jit(solution)/shard_map/reduce_scatter | solution.py:68
  58.3 73.5 %copy-start.5 = (bf16[1,1,64,2,32,256]{5,4,3,2,1,0:T(8,128)(2,1)S(1)}, bf16[1,1,64,2,32,256]{5,4,3,2,1,0:T(8,128)(2,1)}, u32[]{:S(2)}) copy-start(bf16[1,1,64,2,32,256]{5,4,3,2,1,0:T(8,128)(2,1)} %param.13) | copy-start | bytes 6291460
  58.4 107.8 %all-gather.2.cloned.1.call-start = ((), (), s32[]{:S(2)}) async-start(), calls=%async_computation.5 | async-start | bytes 5242880 | tf_op jit(solution)/shard_map/all_gather | solution.py:71
  131.6 190.8 %reduce-scatter.5.cloned.1.call-start = ((), (), s32[]{:S(2)}) async-start(), calls=%async_computation.6 | async-start | bytes 2359296 | tf_op jit(solution)/shard_map/reduce_scatter | solution.py:122
  131.8 2.4 copy-start.6
  135.6 8.1 %copy-start.7 = (s32[1,1,96]{2,1,0:T(1,128)S(1)}, s32[1,1,96]{2,1,0:T(1,128)}, u32[]{:S(2)}) copy-start(s32[1,1,96]{2,1,0:T(1,128)} %param.15) | copy-start | bytes 1156
  193.3 5.9 %copy-start = (bf16[64,256,128]{2,1,0:T(8,128)(2,1)S(1)}, bf16[64,256,128]{2,1,0:T(8,128)(2,1)}, u32[]{:S(2)}) copy-start(bf16[64,256,128]{2,1,0:T(8,128)(2,1)} %gather_fusion.1) | copy-start | bytes 12582916
  199.1 2.0 copy-start.3
  203.5 1.6 copy-start.2
  246.4 4.6 %copy-start.1 = (bf16[96,256,128]{2,0,1:T(8,128)(2,1)S(1)}, bf16[96,256,128]{2,0,1:T(8,128)(2,1)}, u32[]{:S(2)}) copy-start(bf16[96,256,128]{2,0,1:T(8,128)(2,1)} %copy.82) | copy-start | bytes 18874372
Sparse Core Ops, SparseCore 0:
  58.5 70.2 reduce-scatter.2
  131.7 34.4 all-gather.1
  254.1 68.2 reduce-scatter.4
where the time goes:
time: 332 us; the launch traced here: 331 us
  waiting for transfers between devices  186 us (56%)
  local copies, waits for them, and re-layouts  60.1 us (18%)
  matrix products  31.5 us (9%)
  other arithmetic  26.8 us (8%)
  between operations  13.3 us (4%)
  starting transfers between devices  12.7 us (4%)
    reduce_scatter x1, waiting for transfers between devices, per_device(): lax.psum_scatter(cluster_sums, 'row', scatter_dimension=1, tiled=True)  70.3 us
    reduce_scatter x1, waiting for transfers between devices, per_device(): lax.psum_scatter(row_sums, 'col', scatter_dimension=0, tiled=True)  68.5 us
    all_to_all x1, waiting for transfers between devices, per_device(): lax.all_to_all(outgoing, 'col', split_axis=0, concat_axis=0, tiled=True)  24.1 us
    all_gather x1, waiting for transfers between devices, per_device(): sources = lax.all_gather(source_share, 'row', axis=1, tiled=True)  22.3 us
    unnamed x25, local copies, waits for them, and re-layouts  19.2 us
    convert_element_type x1, local copies, waits for them, and re-layouts, per_device(): low_part = (all_terms - high_part.astype(jnp.float32)).astype(jnp.bfloat16)  9.1 us
    convert_element_type x1, local copies, waits for them, and re-layouts, per_device(): high_part = all_terms.astype(jnp.bfloat16)  9.03 us
    convert_element_type x1, other arithmetic, per_device(): low_part = (all_terms - high_part.astype(jnp.float32)).astype(jnp.bfloat16)  9.01 us
  transfers between devices with their start and end apart: 5, of which 5 were waited for; matrix products, arithmetic and copies ran while one was open for 5% of the time, Pallas kernels for 0%

commit v1 on v0

--- a/solution.py
+++ b/solution.py
@@ -6,6 +6,28 @@
 RC_DEV = 16
 CC_DEV = 64
 NEAR_DEV = 32
+
+
+def measure_lines(x_local, dim_k):
+    x_local = jnp.moveaxis(x_local, 0, dim_k)
+    long_array = x_local.shape
+    return x_local.reshape(
+        *long_array[:dim_k], long_array[dim_k] * long_array[dim_k + 1], *long_array[dim_k + 2 :]
+    )
+
+
+def order_the_tiles(u, mesh_dim):
+    axis_total = jax.lax.axis_size(mesh_dim)
+    r1 = u[None]
+    for d in range(axis_total.bit_length() - 1):
+        local_part = 1 << d
+        piece_next = jax.lax.ppermute(
+            r1, mesh_dim, [(j0, j0 ^ local_part) for j0 in range(axis_total)]
+        )
+        arr_now = jnp.stack([r1, piece_next])
+        g_now = jax.lax.axis_index(mesh_dim) >> d & 1
+        r1 = jnp.where(g_now == 0, arr_now, arr_now[::-1]).reshape(-1, *u.shape)
+    return r1
 
 
 def rotate_blocks(values, load_count):
@@ -68,7 +90,11 @@
     source_share = lax.psum_scatter(cluster_sums, "row", scatter_dimension=1, tiled=True).astype(
         jnp.bfloat16
     )
-    sources = lax.all_gather(source_share, "row", axis=1, tiled=True)
+
+    def scan_works(dim_no, q_in, field_in):
+        return measure_lines(order_the_tiles(field_in, q_in), dim_no)
+
+    sources = scan_works(1, q_in="row", field_in=source_share)
     pair_codes = block_pairs.reshape(-1)
     owners = pair_codes // CC_DEV
     columns = pair_codes % CC_DEV

time: 332 us -> 351 us (1.057)
  waiting for transfers between devices: 186 us -> 202 us
  other arithmetic: 26.8 us -> 32.3 us
    ppermute x0 -> x2, waiting for transfers between devices: none -> 37.8 us  [order_the_tiles(): jax.lax.ppermute(r1, mesh_dim, [(j0, j0 ^ local_part) for j0 in range(axi...]
    all_gather x1 -> x0, waiting for transfers between devices: 22.3 us -> none  [per_device(): sources = lax.all_gather(source_share, 'row', axis=1, tiled=True)]
    another operation x0 -> x4, other arithmetic: none -> 6.9 us  [order_the_tiles(): arr_now = jnp.stack([r1, piece_next])]
    all_gather x1 -> x0, local copies, waits for them, and re-layouts: 6.82 us -> none  [per_device(): sources = lax.all_gather(source_share, 'row', axis=1, tiled=True)]
    transpose x0 -> x1, local copies, waits for them, and re-layouts: none -> 4.64 us  [measure_lines(): x_local = jnp.moveaxis(x_local, 0, dim_k)]
    unnamed x25 -> x23, local copies, waits for them, and re-layouts: 19.2 us -> 19.7 us
  transfers between devices with their start and end apart: 5 -> 6, of which waited for: 5 -> 6; matrix products, arithmetic and copies ran while one was open for 5% -> 5% of each run, Pallas kernels for 0% -> 0%
where the time goes in v1:
time: 351 us; the launch traced here: 350 us
  waiting for transfers between devices  202 us (58%)
  local copies, waits for them, and re-layouts  58.3 us (17%)
  other arithmetic  32.3 us (9%)
  matrix products  31.5 us (9%)
  between operations  13.6 us (4%)
  starting transfers between devices  13.1 us (4%)
    reduce_scatter x1, waiting for transfers between devices, per_device(): lax.psum_scatter(cluster_sums, 'row', scatter_dimension=1, tiled=True)  70.1 us
    reduce_scatter x1, waiting for transfers between devices, per_device(): lax.psum_scatter(row_sums, 'col', scatter_dimension=0, tiled=True)  68.6 us
    ppermute x2, waiting for transfers between devices, order_the_tiles(): jax.lax.ppermute(r1, mesh_dim, [(j0, j0 ^ local_part) for j0 in range(axi...  37.8 us
    all_to_all x1, waiting for transfers between devices, per_device(): lax.all_to_all(outgoing, 'col', split_axis=0, concat_axis=0, tiled=True)  24.1 us
    unnamed x23, local copies, waits for them, and re-layouts  19.7 us
    convert_element_type x1, local copies, waits for them, and re-layouts, per_device(): low_part = (all_terms - high_part.astype(jnp.float32)).astype(jnp.bfloat16)  9.1 us
    convert_element_type x1, local copies, waits for them, and re-layouts, per_device(): high_part = all_terms.astype(jnp.bfloat16)  9.03 us
    convert_element_type x1, other arithmetic, per_device(): low_part = (all_terms - high_part.astype(jnp.float32)).astype(jnp.bfloat16)  9.01 us
  transfers between devices with their start and end apart: 6, of which 6 were waited for; matrix products, arithmetic and copies ran while one was open for 5% of the time, Pallas kernels for 0%

profile of v1, /device:TPU:0, one launch (start us, length us, event | category | flops | bytes accessed | tf_op | source)
XLA Modules:
  0.0 350.5 jit_solution(88871660595949437)
XLA Ops:
  6.5 0.8 broadcast_add_fusion
  7.4 0.1 copy.59
  7.5 0.1 add.78
  7.5 0.8 copy.58
  8.3 0.1 reshape.93
  8.4 0.1 fusion.32
  8.5 0.2 select_reduce_fusion.1
  8.7 0.1 select_reduce_fusion
  8.8 0.7 sub.20
  9.5 7.3 %all-to-all-start = ((s32[8,1,2]{2,1,0:T(1,128)}), s32[8,1,2]{2,1,0:T(1,128)S(1)}, u32[]{:S(2)}, u32[]{:S(2)}) async-start(s32[8,1,2]{2,1,0:T(1,128)} %bitcast.2), calls=%async_computation | async-start | bytes 8192 | tf_op jit(solution)/shard_map/all_to_all | solution.py:80
  16.8 1.2 fusion.48
  17.9 0.1 copy.82
  18.1 0.1 copy.83
  18.3 1.7 fusion.22
  20.0 0.5 fusion.10
  20.4 0.7 fusion.13
  21.1 1.2 copy.89
  22.3 0.9 all-to-all-done
  23.2 5.1 %all-to-all-start.1 = ((bf16[8,2,256,128]{3,2,1,0:T(8,128)(2,1)}), bf16[8,2,256,128]{3,2,1,0:T(8,128)(2,1)S(1)}, u32[]{:S(2)}, u32[]{:S(2)}) async-start(bf16[8,2,256,128]{3,2,1,0:T(8,128)(2,1)} %bitcast.48), calls=%async_computation.1 | async-start | bytes 2097152 | tf_op jit(solution)/shard_map/all_to_all | solution.py:79
  28.3 0.5 broadcast.109
  28.9 0.7 reduce.3
  29.5 0.1 eq.74
  29.6 24.1 %all-to-all-done.1 = bf16[8,2,256,128]{3,2,1,0:T(8,128)(2,1)S(1)} async-done(((bf16[8,2,256,128]{3,2,1,0:T(8,128)(2,1)}), bf16[8,2,256,128]{3,2,1,0:T(8,128)(2,1)S(1)}, u32[]{:S(2)}, u32[]{:S(2)}) %all-to-all-start.1) | async-done | bytes 1048608 | tf_op jit(solution)/shard_map/all_to_all | solution.py:79
  53.7 4.6 %fusion.17 = f32[64,256,128]{2,0,1:T(8,128)} fusion(s32[16]{0:T(128)S(1)} %eq.74, bf16[2,8,256,128]{3,2,1,0:T(8,128)(2,1)S(1)} %bitcast.136), kind=kOutput, calls=%fused_computation.38 | convolution fusion | flops 67109888 | bytes 9437248 | tf_op jit(solution)/shard_map/dot_general | solution.py:85
  58.3 0.2 reduce-scatter.5.cloned.1.call-start
  58.6 70.1 %reduce-scatter.3.cloned.1.call-done = f32[64,64,128]{2,0,1:T(8,128)} async-done(((f32[64,256,128]{2,0,1:T(8,128)}), f32[64,64,128]{2,0,1:T(8,128)}) %reduce-scatter.3.cloned.1.call-update) | async-done | bytes 2097168 | tf_op jit(solution)/shard_map/reduce_scatter | solution.py:90
  128.7 2.1 convert_bitcast_fusion.1
  131.0 2.6 collective-permute-done
  133.6 0.2 pad_maximum_fusion.2
  133.8 2.6 fusion.12
  136.4 0.3 collective-permute-start.1
  136.7 3.3 copy.107
  140.0 1.5 copy.106
  141.5 7.6 %copy.105 = bf16[1,1,32,2,256,256]{5,4,2,3,1,0:T(8,128)(2,1)} copy(bf16[1,1,32,2,256,256]{5,4,3,2,1,0:T(8,128)(2,1)} %param.12) | data formatting | bytes 16777216 | tf_op args[4]
  149.2 0.1 compare_select_fusion
  149.2 35.1 %collective-permute-done.1 = bf16[2,64,64,128]{3,1,2,0:T(8,128)(2,1)} collective-permute-done((bf16[2,64,64,128]{3,1,2,0:T(8,128)(2,1)}, bf16[2,64,64,128]{3,1,2,0:T(8,128)(2,1)}, u32[]{:S(2)}, u32[]{:S(2)}) %collective-permute-start.1) | collective-permute-done | bytes 2097184 | tf_op jit(solution)/shard_map/ppermute | solution.py:24
  184.4 2.0 pad_maximum_fusion.1
  186.4 1.7 reverse_select_fusion
  188.0 4.6 %copy.67 = bf16[64,4,64,128]{3,2,1,0:T(8,128)(2,1)} copy(bf16[64,4,64,128]{3,0,2,1:T(8,128)(2,1)S(1)} %bitcast.128) | data formatting | bytes 8388608 | tf_op jit(solution)/shard_map/transpose | solution.py:12
  192.7 3.1 gather_fusion
  195.8 5.2 %gather_fusion.1 = bf16[64,256,128]{2,1,0:T(8,128)(2,1)} fusion(bf16[64,256,128]{2,1,0:T(8,128)(2,1)} %bitcast.127, s32[1024]{0:T(1024)S(1)} %pad_clamp_fusion), kind=kCustom, calls=%fused_computation.1 | custom fusion | bytes 8388864 | tf_op jit(solution)/shard_map/gather | solution.py:112
  201.1 2.9 fusion.47
  203.9 1.9 copy.85
  205.8 1.2 neg.13
  207.0 1.9 copy.86
  208.9 4.0 %fusion.1 = f32[32,128,256]{2,1,0:T(8,128)S(1)} fusion(bf16[32,2,256,256]{3,2,0,1:T(8,128)(2,1)} %bitcast.124, bf16[32,256,64]{1,2,0:T(8,128)(2,1)S(1)} %copy.86, bf16[32,256,64]{1,2,0:T(8,128)(2,1)} %neg.13), kind=kOutput, calls=%fused_computation.11 | convolution fusion | flops 541065216 | bytes 10485760 | tf_op jit(solution)/shard_map/dym,dmg->dyg/dot_general | solution.py:106
  213.0 5.8 %add_bitcast_fusion.1 = f32[32,256,128]{1,2,0:T(8,128)} fusion(f32[32,128,256]{2,1,0:T(8,128)S(1)} %fusion.1, bf16[32,256,128]{2,1,0:T(8,128)(2,1)S(1)} %gather_fusion, bf16[32,2,256,256]{3,2,0,1:T(8,128)(2,1)} %bitcast.125), kind=kOutput, calls=%fused_computation.19 | convolution fusion | flops 537919488 | bytes 14680064 | tf_op jit(solution)/shard_map/dym,dmg->dyg/dot_general | solution.py:103
  218.8 1.8 slice_negate_fusion
  220.6 2.3 fusion.3
  222.9 0.8 fusion.14
  223.8 0.2 slice_negate_fusion.1
  224.0 0.5 copy-done.2
  224.5 1.3 fusion.20
  225.8 5.0 %add_bitcast_fusion = f32[64,256,128]{1,2,0:T(8,128)} fusion(f32[64,128,256]{2,1,0:T(8,128)S(1)} %fusion.20, bf16[64,2,32,256]{3,2,0,1:T(8,128)(2,1)S(1)} %bitcast.130, bf16[64,32,64]{2,1,0:T(8,128)(2,1)S(1)} %get-tuple-element.14, bf16[64,32,64]{2,1,0:T(8,128)(2,1)S(1)} %get-tuple-element.13), kind=kOutput, calls=%fused_computation.7 | convolution fusion | flops 137363456 | bytes 18874368 | tf_op jit(solution)/shard_map/brp,brk->bpk/dot_general | solution.py:131
  230.9 9.0 %subtract_convert_fusion = bf16[96,256,128]{1,2,0:T(8,128)(2,1)} fusion(f32[64,256,128]{1,2,0:T(8,128)} %add_bitcast_fusion, f32[32,256,128]{1,2,0:T(8,128)} %add_bitcast_fusion.1), kind=kLoop, calls=%fused_computation.4 | loop fusion | flops 15728640 | bytes 18874368 | tf_op jit(solution)/shard_map/convert_element_type | solution.py:139
  239.9 7.9 %fusion = bf16[96,256,128]{1,2,0:T(8,128)(2,1)} fusion(f32[64,256,128]{1,2,0:T(8,128)} %add_bitcast_fusion, f32[32,256,128]{1,2,0:T(8,128)} %add_bitcast_fusion.1), kind=kLoop, calls=%fused_computation.5 | loop fusion | flops 3145728 | bytes 18874368 | tf_op jit(solution)/shard_map/convert_element_type | solution.py:138
  247.7 9.0 %copy.74 = bf16[96,256,128]{2,0,1:T(8,128)(2,1)} copy(bf16[96,256,128]{1,2,0:T(8,128)(2,1)} %fusion) | data formatting | bytes 12582912 | tf_op jit(solution)/shard_map/convert_element_type | solution.py:138
  256.7 9.1 %copy.75 = bf16[96,256,128]{2,0,1:T(8,128)(2,1)} copy(bf16[96,256,128]{1,2,0:T(8,128)(2,1)} %subtract_convert_fusion) | data formatting | bytes 12582912 | tf_op jit(solution)/shard_map/convert_element_type | solution.py:139
  265.9 3.9 %fusion.35 = f32[16,256,128]{2,0,1:T(8,128)S(1)} fusion(bf16[96,256,128]{2,0,1:T(8,128)(2,1)} %copy.74, s32[96]{0:T(128)S(1)} %get-tuple-element.17), kind=kOutput, calls=%fused_computation.69 | convolution fusion | flops 100664832 | bytes 8388992 | tf_op jit(solution)/shard_map/ib,bpk->ipk/dot_general | solution.py:143
  269.7 0.7 copy-done.1
  270.4 0.9 convolution_add_fusion
  271.4 2.0 copy.76
  273.4 68.6 %reduce-scatter.5.cloned.1.call-done = f32[512,128]{1,0:T(8,128)} async-done(((f32[4096,128]{1,0:T(8,128)}), f32[512,128]{1,0:T(8,128)}) %reduce-scatter.5.cloned.1.call-update) | async-done | bytes 262160 | tf_op jit(solution)/shard_map/reduce_scatter | solution.py:148
  342.0 1.6 convert_element_type.43
  (24 shorter events, 0.3 us)
Async XLA Ops:
  6.5 13.4 %copy-start.4 = (bf16[8,2,2,256,128]{4,3,2,1,0:T(8,128)(2,1)S(1)}, bf16[8,2,2,256,128]{4,3,2,1,0:T(8,128)(2,1)}, u32[]{:S(2)}) copy-start(bf16[8,2,2,256,128]{4,3,2,1,0:T(8,128)(2,1)} %param.9) | copy-start | bytes 6291460
  9.5 13.7 %all-to-all-start = ((s32[8,1,2]{2,1,0:T(1,128)}), s32[8,1,2]{2,1,0:T(1,128)S(1)}, u32[]{:S(2)}, u32[]{:S(2)}) async-start(s32[8,1,2]{2,1,0:T(1,128)} %bitcast.2), calls=%async_computation | async-start | bytes 8192 | tf_op jit(solution)/shard_map/all_to_all | solution.py:80
  23.2 30.5 %all-to-all-start.1 = ((bf16[8,2,256,128]{3,2,1,0:T(8,128)(2,1)}), bf16[8,2,256,128]{3,2,1,0:T(8,128)(2,1)S(1)}, u32[]{:S(2)}, u32[]{:S(2)}) async-start(bf16[8,2,256,128]{3,2,1,0:T(8,128)(2,1)} %bitcast.48), calls=%async_computation.1 | async-start | bytes 2097152 | tf_op jit(solution)/shard_map/all_to_all | solution.py:79
  28.3 100.4 %reduce-scatter.3.cloned.1.call-start = ((), (), s32[]{:S(2)}) async-start(), calls=%async_computation.4 | async-start | bytes 10485760 | tf_op jit(solution)/shard_map/reduce_scatter | solution.py:90
  58.3 283.7 %reduce-scatter.5.cloned.1.call-start = ((), (), s32[]{:S(2)}) async-start(), calls=%async_computation.5 | async-start | bytes 2359296 | tf_op jit(solution)/shard_map/reduce_scatter | solution.py:148
  130.9 2.7 collective-permute-start
  136.4 48.0 %collective-permute-start.1 = (bf16[2,64,64,128]{3,1,2,0:T(8,128)(2,1)}, bf16[2,64,64,128]{3,1,2,0:T(8,128)(2,1)}, u32[]{:S(2)}, u32[]{:S(2)}) collective-permute-start(bf16[2,64,64,128]{3,1,2,0:T(8,128)(2,1)} %get-tuple-element.10), channel_id=1, source_target_pairs={{0,16},{8,24},{16,0},{24,8},{1,17},{9,25},{17,1},{25,9},{2,18},{10... | collective-permute-start | bytes 6291464 | tf_op jit(solution)/shard_map/ppermute | solution.py:24
  136.7 3.3 copy-start.5
  141.5 7.6 %copy-start.6 = (s32[1,1,96]{2,1,0:T(1,128)S(1)}, s32[1,1,96]{2,1,0:T(1,128)}, u32[]{:S(2)}) copy-start(s32[1,1,96]{2,1,0:T(1,128)} %param.15) | copy-start | bytes 1156
  213.0 5.8 %copy-start = (bf16[64,256,128]{2,1,0:T(8,128)(2,1)S(1)}, bf16[64,256,128]{2,1,0:T(8,128)(2,1)}, u32[]{:S(2)}) copy-start(bf16[64,256,128]{2,1,0:T(8,128)(2,1)} %gather_fusion.1) | copy-start | bytes 12582916
  218.8 1.8 copy-start.3
  222.9 1.6 copy-start.2
  265.9 4.6 %copy-start.1 = (bf16[96,256,128]{2,0,1:T(8,128)(2,1)S(1)}, bf16[96,256,128]{2,0,1:T(8,128)(2,1)}, u32[]{:S(2)}) copy-start(bf16[96,256,128]{2,0,1:T(8,128)(2,1)} %copy.75) | copy-start | bytes 18874372
Sparse Core Ops, SparseCore 0:
  58.5 70.2 reduce-scatter.2
  273.5 68.4 reduce-scatter.4
